TPU v7x, 128 devices: a whole 4x4x4 slice. The times are simulated.
128 devices in a mesh: seq: 16 (over y, z_lo, core), tp: 8 (over z_hi, x).
Axes of the slice: x: 4, y: 4, z: 4 (z_hi: 2, z_lo: 2; z = z_hi * 2 + z_lo), core: 2. Of those that a mesh axis runs over, the one named last changes fastest.
Arguments:
- tokens: bfloat16 [8192, 2048], P('seq'), may hold values from -6 to 6
- w_zx: float32 [2048, 8192], P(('seq', 'tp')), may hold values from -0.125 to 0.125
- w_dt: float32 [2048, 64], P(('seq', 'tp')), may hold values from -0.26516503 to 0.26516503
- w_bc: float32 [2048, 256], P(('seq', 'tp')), may hold values from -0.125 to 0.125
- conv_x_weight: float32 [4, 4096], P(None, 'tp'), may hold values from -3 to 3
- conv_x_bias: float32 [4096], P('tp'), may hold values from -1.8 to 1.8
- conv_bc_weight: float32 [4, 256], replicated, may hold values from -3 to 3
- conv_bc_bias: float32 [256], replicated, may hold values from -1.8 to 1.8
- dt_bias: float32 [64], P('tp'), may hold values from -11 to -2
- a_log: float32 [64], P('tp'), may hold values from 0 to 2.77
- skip: float32 [64], P('tp'), may hold values from 0.5 to 2
- norm_weight: float32 [4096], P('tp'), may hold values from 0.1 to 1.9
- w_out: float32 [4096, 2048], P('tp', 'seq'), may hold values from -0.09375 to 0.09375
- lengths: int32 [8], replicated, may hold values from 1 to 4096, 8192 in all
- request_group: int32 [32], replicated, may hold values from 0 to 31
Outputs:
- mixed: bfloat16 [8192, 2048], P(('seq', 'tp'))
- request_states: float32 [32, 64, 64, 128], P('seq', 'tp')
Inputs may be any that keep to these rules, and one draw needn't show every extreme that they name: 8 prompts packed end to end in this order; the lengths sum to 8192 and the longest is exactly 4096.
All inputs are finite; a program needn't handle non-finite values.
Results may differ from a plain program's by a relative error of at most 0.011.
Values may be sent and summed in bfloat16 or wider, within the bound.
A program may use at most 128 MiB of HBM per device.

v0:
```python
import jax
import jax.numpy as jnp
from jax import lax
from jax.sharding import PartitionSpec as P

INNER = 4096
GROUP = 256
epsilon = 1e-05


def from_behind(x, axis, by):
    count = lax.axis_size(axis)
    pairs = [(i, i + by) for i in range(count) if 0 <= i + by < count]
    return lax.ppermute(x, axis, pairs)


def segment_of(position, lengths):
    prompt_ends = jnp.cumsum(lengths)
    return jnp.sum((position[:, None] >= prompt_ends[None, :]).astype(jnp.int32), axis=1)


def round_up(n, m):
    return (n + m - 1) // m * m


def on_device(
    tokens,
    w_zx,
    w_dt,
    w_bc,
    conv_x_weight,
    conv_x_bias,
    conv_bc_weight,
    conv_bc_bias,
    dt_bias,
    a_log,
    skip,
    norm_weight,
    w_out,
    lengths,
    request_group,
):
    tp_count = lax.axis_size("tp")
    seq_count = lax.axis_size("seq")
    seq_index = lax.axis_index("seq")
    tok_dev = tokens.shape[0]
    local_rows = w_zx.shape[0]
    inner_local = conv_x_weight.shape[1]
    heads_local = dt_bias.shape[0]
    head_width = inner_local // heads_local
    bc_width = conv_bc_weight.shape[1]
    state_width = bc_width // 2
    taps = conv_x_weight.shape[0]
    groups_dev = tok_dev // GROUP
    zx_part = w_zx.astype(jnp.bfloat16).reshape(local_rows, 2, tp_count, inner_local)
    zx_part = zx_part.transpose(0, 2, 1, 3).reshape(local_rows, tp_count, 2 * inner_local)
    bc_part = jnp.broadcast_to(
        w_bc.astype(jnp.bfloat16)[:, None, :], (local_rows, tp_count, bc_width)
    )
    dt_part = w_dt.astype(jnp.bfloat16).reshape(local_rows, tp_count, heads_local)
    used = 2 * inner_local + bc_width + heads_local
    width = round_up(used, 128)
    pad_part = jnp.zeros((local_rows, tp_count, width - used), jnp.bfloat16)
    packed = jnp.concatenate([zx_part, bc_part, dt_part, pad_part], axis=2)
    packed = packed.reshape(local_rows, tp_count * width)
    block = lax.all_to_all(packed, "tp", split_axis=1, concat_axis=0, tiled=True)
    out_rows, out_cols = w_out.shape
    block_rows = block.shape[0]
    out_piece = w_out.astype(jnp.bfloat16).reshape(block_rows, out_rows * out_cols // block_rows)
    gathered = lax.all_gather(
        jnp.concatenate([block, out_piece], axis=1), "seq", axis=0, tiled=True
    )
    weights = gathered[:, :width]
    out_block = gathered[:, width:].reshape(seq_count, out_rows, out_cols)
    out_block = out_block.transpose(1, 0, 2).reshape(out_rows, seq_count * out_cols)
    proj = jnp.dot(tokens, weights, preferred_element_type=jnp.float32)
    zx_low = proj[:, : 2 * inner_local].astype(jnp.bfloat16)
    gate_z = zx_low[:, :inner_local]
    x_raw = zx_low[:, inner_local:]
    bc_raw = proj[:, 2 * inner_local : 2 * inner_local + bc_width].astype(jnp.bfloat16)
    dt_pre = proj[:, 2 * inner_local + bc_width : used]
    raw_mix = jnp.concatenate([x_raw, bc_raw], axis=1)
    conv_weight = jnp.concatenate([conv_x_weight, conv_bc_weight], axis=1)
    conv_bias = jnp.concatenate([conv_x_bias, conv_bc_bias], axis=0)
    rim_rows = from_behind(raw_mix[tok_dev - (taps - 1) :], "seq", 1)
    padded = jnp.concatenate([rim_rows, raw_mix], axis=0)
    offset = seq_index * tok_dev
    seg_pad = segment_of(
        offset - (taps - 1) + jnp.arange(tok_dev + taps - 1, dtype=jnp.int32), lengths
    )
    seg_tok = seg_pad[taps - 1 :]
    conv_sum = jnp.zeros((tok_dev, raw_mix.shape[1]), jnp.float32) + conv_bias[None, :]
    for offset_tap in range(taps):
        rows_wide = padded[offset_tap : offset_tap + tok_dev].astype(jnp.float32)
        keep_tap = seg_pad[offset_tap : offset_tap + tok_dev] == seg_tok
        conv_sum = conv_sum + jnp.where(
            keep_tap[:, None], rows_wide * conv_weight[offset_tap][None, :], 0.0
        )
    convolved = jax.nn.silu(conv_sum).astype(jnp.bfloat16)
    inputs = convolved[:, :inner_local].reshape(groups_dev, GROUP, heads_local, head_width)
    b_matrix = convolved[:, inner_local : inner_local + state_width].reshape(
        groups_dev, GROUP, state_width
    )
    c_matrix = convolved[:, inner_local + state_width :].reshape(groups_dev, GROUP, state_width)
    step_size = jax.nn.softplus(dt_pre + dt_bias[None, :]).reshape(groups_dev, GROUP, heads_local)
    step_heads = step_size.transpose(0, 2, 1)
    decay_rate = -jnp.exp(a_log)
    cumul_heads = jnp.cumsum(step_size * decay_rate[None, None, :], axis=1).transpose(0, 2, 1)
    segments = seg_tok.reshape(groups_dev, GROUP)
    seg_before = segment_of(offset + jnp.arange(groups_dev, dtype=jnp.int32) * GROUP - 1, lengths)
    within = jnp.arange(GROUP, dtype=jnp.int32)
    same_prompt = (segments[:, :, None] == segments[:, None, :]) & (
        within[:, None] >= within[None, :]
    )[None]
    log_decay = cumul_heads[:, :, :, None] - cumul_heads[:, :, None, :]
    decay_matrix = jnp.where(
        same_prompt[:, None], jnp.exp(jnp.where(same_prompt[:, None], log_decay, 0.0)), 0.0
    )
    scores = jnp.einsum("cin,cjn->cij", c_matrix, b_matrix, preferred_element_type=jnp.float32)
    mix_weights = (decay_matrix * scores[:, None] * step_heads[:, :, None, :]).astype(jnp.bfloat16)
    diag_out = jnp.einsum(
        "chij,cjhp->cihp", mix_weights, inputs, preferred_element_type=jnp.float32
    )
    last_segment = segments[:, -1]
    tail_weight = (
        jnp.where(
            (segments == last_segment[:, None])[:, None, :],
            jnp.exp(cumul_heads[:, :, -1:] - cumul_heads),
            0.0,
        )
        * step_heads
    )
    b_weighted = (b_matrix.astype(jnp.float32)[:, None] * tail_weight[:, :, :, None]).astype(
        jnp.bfloat16
    )
    contrib = jnp.einsum("cjhp,chjn->chpn", inputs, b_weighted, preferred_element_type=jnp.float32)
    pass_gate = jnp.where(
        (last_segment == seg_before)[:, None], jnp.exp(cumul_heads[:, :, -1]), 0.0
    )

    def local_step(carry_state, group_item):
        factor, source = group_item
        next_state = factor[:, None, None] * carry_state + source
        return (next_state, (carry_state, next_state))

    zero_state = jnp.zeros((heads_local, head_width, state_width), jnp.float32)
    _, (local_in, local_end) = lax.scan(local_step, zero_state, (pass_gate, contrib))
    through_group = jnp.cumprod(pass_gate, axis=0)
    before_group = jnp.concatenate(
        [jnp.ones((1, heads_local), jnp.float32), through_group[:-1]], axis=0
    )
    gate_hi = through_group.astype(jnp.bfloat16)
    gate_lo = (through_group - gate_hi.astype(jnp.float32)).astype(jnp.bfloat16)
    extra = jnp.zeros((groups_dev, heads_local, 8, state_width), jnp.bfloat16)
    extra = extra.at[:, :, 0, :].set(
        jnp.broadcast_to(gate_hi[:, :, None], gate_hi.shape + (state_width,))
    )
    extra = extra.at[:, :, 1, :].set(
        jnp.broadcast_to(gate_lo[:, :, None], gate_lo.shape + (state_width,))
    )
    sendable = jnp.concatenate([local_end.astype(jnp.bfloat16), extra], axis=2)
    every = lax.all_gather(sendable, "seq", axis=0, tiled=False)
    every_end = every[:, :, :, :head_width].astype(jnp.float32)
    every_gate = every[:, :, :, head_width, 0].astype(jnp.float32) + every[
        :, :, :, head_width + 1, 0
    ].astype(jnp.float32)
    dev_gate = every_gate[:, -1]
    dev_ids = jnp.arange(seq_count, dtype=jnp.int32)

    def carry_weights(k):
        between = (dev_ids[:, None] < dev_ids[None, :]) & (dev_ids[None, :] < k)
        factors = jnp.where(between[:, :, None], dev_gate[None, :, :], 1.0)
        return jnp.where((dev_ids < k)[:, None], jnp.prod(factors, axis=1), 0.0)

    own_weights = carry_weights(seq_index)
    slot_ids = jnp.arange(groups_dev, dtype=jnp.int32)
    last_slot = (slot_ids == groups_dev - 1).astype(jnp.float32)
    own_coef = own_weights[:, None, :] * last_slot[None, :, None]
    carried = jnp.einsum(
        "jch,jchpn->hpn",
        own_coef,
        every_end,
        precision=lax.Precision.HIGHEST,
        preferred_element_type=jnp.float32,
    )
    group_in = before_group[:, :, None, None] * carried[None] + local_in
    state_low = group_in.astype(jnp.bfloat16)
    carry_keep = jnp.where((segments == seg_before[:, None])[:, None, :], jnp.exp(cumul_heads), 0.0)
    carry_out = jnp.einsum(
        "cin,chpn->cihp", c_matrix, state_low, preferred_element_type=jnp.float32
    )
    carry_out = carry_out * carry_keep.transpose(0, 2, 1)[:, :, :, None]
    y_local = diag_out + carry_out + skip[None, None, :, None] * inputs.astype(jnp.float32)
    y_local = y_local.reshape(tok_dev, inner_local)
    gated = y_local * jax.nn.silu(gate_z.astype(jnp.float32))
    square_sum = jnp.sum(gated * gated, axis=1)
    scaled = (gated * norm_weight[None, :]).astype(jnp.bfloat16)
    partial = jnp.dot(scaled, out_block, preferred_element_type=jnp.float32)
    side = jnp.zeros((tok_dev, 128), jnp.float32).at[:, 0].set(square_sum)
    summed = lax.psum_scatter(
        jnp.concatenate([partial, side], axis=1).astype(jnp.bfloat16),
        "tp",
        scatter_dimension=0,
        tiled=True,
    ).astype(jnp.float32)
    d_model = out_block.shape[1]
    mean_square = summed[:, d_model] / INNER
    mixed = (summed[:, :d_model] * lax.rsqrt(mean_square + epsilon)[:, None]).astype(jnp.bfloat16)
    req_dev = request_group.shape[0] // seq_count
    mine = lax.dynamic_slice_in_dim(request_group, seq_index * req_dev, req_dev)
    req_k = mine // groups_dev
    req_c = mine % groups_dev
    req_w = jax.vmap(carry_weights)(req_k)
    req_gate = every_gate[req_k, req_c]
    coef = req_gate[:, None, None, :] * req_w[:, :, None, :] * last_slot[None, None, :, None]
    hit = (dev_ids[None, :, None] == req_k[:, None, None]) & (
        slot_ids[None, None, :] == req_c[:, None, None]
    )
    coef = coef + hit[:, :, :, None].astype(jnp.float32)
    request_states = jnp.einsum(
        "rjch,jchpn->rhpn",
        coef,
        every_end,
        precision=lax.Precision.HIGHEST,
        preferred_element_type=jnp.float32,
    )
    return (mixed.astype(jnp.bfloat16), request_states)


def solution(mesh):
    return jax.shard_map(
        on_device,
        mesh=mesh,
        in_specs=(
            P("seq", None),
            P(("seq", "tp"), None),
            P(("seq", "tp"), None),
            P(("seq", "tp"), None),
            P(None, "tp"),
            P("tp"),
            P(),
            P(),
            P("tp"),
            P("tp"),
            P("tp"),
            P("tp"),
            P("tp", "seq"),
            P(),
            P(),
        ),
        out_specs=(P(("seq", "tp"), None), P("seq", "tp", None, None)),
        check_vma=False,
    )
```

profile of v0, /device:TPU:0, one launch (start us, length us, event | category | flops | bytes accessed | tf_op | source)
XLA Modules:
  0.0 252.9 jit_solution(9752416855945971542)
XLA Ops:
  7.2 0.9 convert_element_type.126
  8.1 0.8 copy.117
  9.0 1.1 convert_element_type.125
  10.6 0.8 concatenate.38
  11.4 7.7 %all-to-all-start = ((bf16[16,8,1408]{2,0,1:T(8,128)(2,1)}), bf16[16,8,1408]{2,0,1:T(8,128)(2,1)S(1)}, u32[]{:S(2)}, u32[]{:S(2)}) async-start(bf16[16,8,1408]{2,0,1:T(8,128)(2,1)} %concatenate.38), calls=%async_computation | async-start | bytes 720896 | tf_op jit(solution)/shard_map/all_to_all | solution.py:66
  19.3 9.7 %all-to-all-done = bf16[16,8,1408]{2,0,1:T(8,128)(2,1)S(1)} async-done(((bf16[16,8,1408]{2,0,1:T(8,128)(2,1)}), bf16[16,8,1408]{2,0,1:T(8,128)(2,1)S(1)}, u32[]{:S(2)}, u32[]{:S(2)}) %all-to-all-start) | async-done | bytes 360480 | tf_op jit(solution)/shard_map/all_to_all | solution.py:66
  29.0 0.8 pad_maximum_fusion.1
  32.9 44.3 %all-gather.4.cloned.1.call-done = bf16[2048,1920]{1,0:T(8,128)(2,1)} async-done(((bf16[128,1920]{1,0:T(8,128)(2,1)}), bf16[2048,1920]{1,0:T(8,128)(2,1)}) %all-gather.4.cloned.1.call-update) | async-done | bytes 7864336 | tf_op jit(solution)/shard_map/all_gather | solution.py:70
  77.2 7.0 %fusion.65 = (bf16[512,1408]{0,1:T(8,128)(2,1)}, f32[512,1408]{0,1:T(8,128)S(1)}) fusion(bf16[512,2048]{1,0:T(8,128)(2,1)S(1)} %copy-done, bf16[2048,1920]{1,0:T(8,128)(2,1)} %all-gather.4.cloned.1.call-done), kind=kOutput, calls=%fused_computation.143 | convolution fusion | flops 2953510912 | bytes 12189696 | tf_op jit(solution)/shard_map/dot_general | solution.py:76
  84.4 1.1 reduce-window.19
  85.7 0.7 select_bitcast_fusion
  86.5 1.0 slice.203
  87.6 2.2 collective-permute-start
  89.9 0.7 select_multiply_fusion.1
  90.6 1.2 slice.204
  92.5 0.7 broadcast.361
  93.2 1.4 scatter.11
  94.5 2.9 %multiply_convert_fusion.3 = bf16[512,768]{0,1:T(8,128)(2,1)S(1)} fusion(bf16[512,768]{0,1:T(8,128)(2,1)S(1)} %slice.204, bf16[3,768]{0,1:T(8,128)(2,1)S(1)} %collective-permute-done, f32[768]{0:T(1024)} %get-tuple-element.107, f32[768]{0:T(1024)} %get-tuple-element.108, f32[768]{0:T(1024)} %get-tuple-element.109, f32[768]{0:T(1024)} %get-tuple-element.106, ...), kind=kLoop, calls=%fused_computation.26 | loop fusion | flops 11403264 | bytes 1594368 | tf_op jit(solution)/shard_map/convert_element_type | solution.py:99
  97.5 0.7 fusion.64
  98.3 0.9 reshape.472
  99.2 0.8 copy.124
  100.1 2.0 fusion.29
  102.0 2.9 %while.18 = (s32[]{:T(128)}, f32[8,64,128]{2,1,0:T(8,128)S(1)}, f32[2,8,64,128]{3,2,1,0:T(8,128)}, bf16[2,8,64,128]{3,2,1,0:T(8,128)(2,1)}, f32[2,8]{1,0:T(2,128...) while((s32[]{:T(128)}, f32[8,64,128]{2,1,0:T(8,128)S(1)}, ...), condition=%wide.region_7.8_spmd.clone, body=%wide.region_6.7_spmd.clone.sunk | while | flops 196611 | bytes 1310927 | solution.py:147
  102.0 0.7 fusion.70
  102.7 0.8 bitcast_dynamic-update-slice_fusion.3
  103.5 0.7 fusion.70
  104.1 0.8 bitcast_dynamic-update-slice_fusion.3
  104.9 1.7 pad_maximum_fusion.2
  106.7 0.7 compare_reduce_fusion
  108.6 1.6 compare_and_fusion
  110.2 3.1 %slice.226 = bf16[2048,512]{1,0:T(8,128)(2,1)} slice(bf16[2048,1920]{1,0:T(8,128)(2,1)} %all-gather.4.cloned.1.call-done), slice={[0:2048], [1408:1920]} | slice | bytes 4194304 | tf_op jit(solution)/shard_map/slice | solution.py:74
  113.3 4.3 %reshape.474 = bf16[16,512,128]{2,1,0:T(8,128)(2,1)} reshape(bf16[2048,512]{1,0:T(8,128)(2,1)} %slice.226) | data formatting | bytes 4194304 | tf_op jit(solution)/shard_map/reshape | solution.py:74
  117.6 4.0 %copy.132 = bf16[16,512,128]{1,2,0:T(8,128)(2,1)} copy(bf16[16,512,128]{2,1,0:T(8,128)(2,1)} %reshape.474) | data formatting | bytes 4194304 | tf_op jit(solution)/shard_map/reshape | solution.py:74
  122.5 3.3 %fusion.19 = f32[2,256,8,64]{1,3,2,0:T(8,128)} fusion(f32[2,8,256]{2,1,0:T(8,128)S(1)} %bitcast.108, f32[2,256,256]{2,1,0:T(8,128)S(1)} %fusion.40, f32[2,8,256]{2,1,0:T(8,128)} %copy-done.7, pred[2,256,256]{2,1,0:T(8,128)(4,1)} %compare_and_fusion, bf16[2,256,8,64]{1,0,3,2:T(2,128)(2,1)S(1)} %reshape.467), kind=kOutput, calls=%fused_computation.27 | convolution fusion | flops 140509184 | bytes 2260992 | tf_op jit(solution)/shard_map/chij,cjhp->cihp/dot_general | solution.py:121
  125.9 21.1 %all-gather.6.cloned.1.call-done = bf16[32,8,72,128]{3,2,1,0:T(8,128)(2,1)} async-done(((bf16[2,8,72,128]{3,2,1,0:T(8,128)(2,1)}), bf16[32,8,72,128]{3,2,1,0:T(8,128)(2,1)}) %all-gather.6.cloned.1.call-update) | async-done | bytes 4718608 | tf_op jit(solution)/shard_map/all_gather | solution.py:162
  147.0 1.5 fusion.63
  148.5 5.7 %slice.224 = bf16[16,2,8,64,128]{4,3,2,1,0:T(8,128)(2,1)} slice(bf16[16,2,8,72,128]{4,3,2,1,0:T(8,128)(2,1)} %bitcast.93), slice={[0:16], [0:2], [0:8], [0:64], [0:128]} | slice | bytes 8388608 | tf_op jit(solution)/shard_map/slice | solution.py:163
  155.2 6.3 %fusion.6 = f32[8,1,64,128,1]{3,1,4,2,0:T(1,128)S(1)} fusion(f32[16,2,8,1,1]{0,3,1,4,2:T(1,128)S(1)} %copy.138, bf16[16,2,8,64,128]{4,3,2,1,0:T(8,128)(2,1)} %slice.224), kind=kOutput, calls=%fused_computation.13 | convolution fusion | flops 25165824 | bytes 4457472 | tf_op jit(solution)/shard_map/jch,jchpn->hpn/dot_general | solution.py:179
  161.9 0.8 copy.131
  163.6 0.6 select_convert_fusion
  164.4 1.6 convolution_convert_fusion
  166.0 1.6 fusion.11
  167.6 0.6 copy-done.22
  169.9 5.8 %fusion.22 = f32[2,8,64,128]{3,0,2,1:T(2,128)S(1)} fusion(bf16[16,2,8,64,128]{4,3,2,1,0:T(8,128)(2,1)} %slice.224, f32[2,16,2]{1,0,2:T(2,128)S(1)} %and_convert_fusion, f32[2,16,8]{1,0,2:T(2,128)S(1)} %copy.135, f32[2]{0:T(128)S(1)} %copy-done.23), kind=kOutput, calls=%fused_computation.35 | convolution fusion | flops 50332672 | bytes 4719880 | tf_op jit(solution)/shard_map/rjch,jchpn->rhpn/dot_general | solution.py:220
  175.7 0.9 copy.136
  176.6 67.9 %reduce-scatter.2.cloned.1.call-done = bf16[64,2176]{1,0:T(8,128)(2,1)} async-done(((bf16[512,2176]{1,0:T(8,128)(2,1)}), bf16[64,2176]{1,0:T(8,128)(2,1)}) %reduce-scatter.2.cloned.1.call-update) | async-done | bytes 278544 | tf_op jit(solution)/shard_map/reduce_scatter | solution.py:200
  244.5 1.0 convert_element_type.149
  245.6 0.8 fusion.34
  (134 shorter events, 11.7 us)
Async XLA Ops:
  7.2 70.0 %copy-start = (bf16[512,2048]{1,0:T(8,128)(2,1)S(1)}, bf16[512,2048]{1,0:T(8,128)(2,1)}, u32[]{:S(2)}) copy-start(bf16[512,2048]{1,0:T(8,128)(2,1)} %param.23) | copy-start | bytes 6291460
  7.2 12.0 %copy-start.6 = (f32[512,128]{1,0:T(8,128)S(1)}, f32[512,128]{1,0:T(8,128)}, u32[]{:S(2)}) copy-start(f32[512,128]{1,0:T(8,128)} %param.35) | copy-start | bytes 786436
  10.3 19.6 %copy-start.25 = (s32[8]{0:T(128)S(1)}, s32[8]{0:T(128)}, u32[]{:S(2)}) copy-start(s32[8]{0:T(128)} %param.36) | copy-start | bytes 100
  10.3 20.4 %copy-start.16 = (f32[512]{0:T(512)S(1)}, f32[512]{0:T(512)}, u32[]{:S(2)}) copy-start(f32[512]{0:T(512)} %param.28) | copy-start | bytes 6148
  10.4 20.4 %copy-start.19 = (f32[256]{0:T(256)S(1)}, f32[256]{0:T(256)}, u32[]{:S(2)}) copy-start(f32[256]{0:T(256)} %param.30) | copy-start | bytes 3076
  10.4 21.0 %copy-start.11 = (f32[4,512]{1,0:T(4,128)S(1)}, f32[4,512]{1,0:T(4,128)}, u32[]{:S(2)}) copy-start(f32[4,512]{1,0:T(4,128)} %param.27) | copy-start | bytes 24580
  10.4 21.0 %copy-start.13 = (f32[4,256]{1,0:T(4,128)S(1)}, f32[4,256]{1,0:T(4,128)}, u32[]{:S(2)}) copy-start(f32[4,256]{1,0:T(4,128)} %param.29) | copy-start | bytes 12292
  10.4 21.8 %copy-start.26 = (f32[8]{0:T(128)S(1)}, f32[8]{0:T(128)}, u32[]{:S(2)}) copy-start(f32[8]{0:T(128)} %param.32) | copy-start | bytes 100
  11.4 17.5 %all-to-all-start = ((bf16[16,8,1408]{2,0,1:T(8,128)(2,1)}), bf16[16,8,1408]{2,0,1:T(8,128)(2,1)S(1)}, u32[]{:S(2)}, u32[]{:S(2)}) async-start(bf16[16,8,1408]{2,0,1:T(8,128)(2,1)} %concatenate.38), calls=%async_computation | async-start | bytes 720896 | tf_op jit(solution)/shard_map/all_to_all | solution.py:66
  19.1 58.0 %all-gather.4.cloned.1.call-start = ((), (), s32[]{:S(2)}) async-start(), calls=%async_computation.2 | async-start | bytes 8355840 | tf_op jit(solution)/shard_map/all_gather | solution.py:70
  29.8 117.1 %all-gather.6.cloned.1.call-start = ((), (), s32[]{:S(2)}) async-start(), calls=%async_computation.4 | async-start | bytes 5013504 | tf_op jit(solution)/shard_map/all_gather | solution.py:162
  30.6 53.6 %copy-start.9 = (s32[2,256]{1,0:T(2,128)}, s32[2,256]{1,0:T(2,128)S(1)}, u32[]{:S(2)}) copy-start(s32[2,256]{1,0:T(2,128)S(1)} %eq.111) | copy-start | bytes 6148
  32.9 51.3 %copy-start.20 = (f32[8]{0:T(128)S(1)}, f32[8]{0:T(128)}, u32[]{:S(2)}) copy-start(f32[8]{0:T(128)} %param.31) | copy-start | bytes 100
  86.4 4.2 %copy-start.7 = (f32[2,8,256]{2,1,0:T(8,128)}, f32[2,8,256]{2,1,0:T(8,128)S(1)}, u32[]{:S(2)}) copy-start(f32[2,8,256]{2,1,0:T(8,128)S(1)} %get-tuple-element.130) | copy-start | bytes 49156
  87.6 6.9 %collective-permute-start = (bf16[3,768]{0,1:T(8,128)(2,1)S(1)}, bf16[3,768]{0,1:T(8,128)(2,1)S(1)}, u32[]{:S(2)}, u32[]{:S(2)}) collective-permute-start(bf16[3,768]{0,1:T(8,128)(2,1)S(1)} %slice.203), channel_id=1, source_target_pairs={{0,8},{8,16},{16,24},{24,32},{32,40},{40,48},{48,56},{56,64},{64,7... | collective-permute-start | bytes 13832 | tf_op jit(solution)/shard_map/ppermute | solution.py:14
  89.8 0.7 copy-start.15
  89.9 0.7 copy-start.14
  106.6 137.8 %reduce-scatter.2.cloned.1.call-start = ((), (), s32[]{:S(2)}) async-start(), calls=%async_computation.3 | async-start | bytes 2506752 | tf_op jit(solution)/shard_map/reduce_scatter | solution.py:200
  107.4 2.8 %copy-start.17 = (pred[16]{0:T(512)(128)(4,1)}, pred[16]{0:T(512)(128)(4,1)S(1)}, u32[]{:S(2)}) copy-start(pred[16]{0:T(512)(128)(4,1)S(1)} %iota_compare_fusion.6) | copy-start | bytes 52
  117.6 4.0 %slice-start = ((f32[2,8]{1,0:T(2,128)}), f32[1,8]{1,0:T(1,128)S(1)}, s32[]{:S(2)}) async-start(f32[2,8]{1,0:T(2,128)} %copy-done.14), calls=%async_computation.5 | async-start | bytes 1024 | tf_op jit(solution)/shard_map/slice | solution.py:150
  117.6 4.6 %copy-start.3 = (bf16[512,128]{0,1:T(8,128)(2,1)S(1)}, bf16[512,128]{0,1:T(8,128)(2,1)}, u32[]{:S(2)}) copy-start(bf16[512,128]{0,1:T(8,128)(2,1)} %get-tuple-element.135) | copy-start | bytes 393220
  148.5 6.1 %copy-start.10 = (pred[16,16]{1,0:T(8,128)(4,1)S(1)}, pred[16,16]{1,0:T(8,128)(4,1)}, u32[]{:S(2)}) copy-start(pred[16,16]{1,0:T(8,128)(4,1)} %broadcast_and_fusion.1) | copy-start | bytes 772
  148.5 6.5 %copy-start.18 = (pred[16]{0:T(512)(128)(4,1)S(1)}, pred[16]{0:T(512)(128)(4,1)}, u32[]{:S(2)}) copy-start(pred[16]{0:T(512)(128)(4,1)} %copy-done.17) | copy-start | bytes 52
  148.5 6.5 %copy-start.23 = (f32[2]{0:T(128)S(1)}, f32[2]{0:T(128)}, u32[]{:S(2)}) copy-start(f32[2]{0:T(128)} %compare_convert_fusion) | copy-start | bytes 28
  155.2 6.3 %copy-start.4 = (f32[2,256,8,64]{1,3,2,0:T(8,128)S(1)}, f32[2,256,8,64]{1,3,2,0:T(8,128)}, u32[]{:S(2)}) copy-start(f32[2,256,8,64]{1,3,2,0:T(8,128)} %fusion.19) | copy-start | bytes 3145732
  155.2 6.3 %copy-start.5 = (f32[2,8,64,128]{3,2,1,0:T(8,128)S(1)}, f32[2,8,64,128]{3,2,1,0:T(8,128)}, u32[]{:S(2)}) copy-start(f32[2,8,64,128]{3,2,1,0:T(8,128)} %get-tuple-element.72) | copy-start | bytes 1572868
  155.2 6.3 %copy-start.8 = (f32[2,256,8]{1,2,0:T(8,128)S(1)}, f32[2,256,8]{1,2,0:T(8,128)}, u32[]{:S(2)}) copy-start(f32[2,256,8]{1,2,0:T(8,128)} %get-tuple-element.129) | copy-start | bytes 49156
  155.2 6.3 %copy-start.12 = (f32[2,8]{1,0:T(2,128)S(1)}, f32[2,8]{1,0:T(2,128)}, u32[]{:S(2)}) copy-start(f32[2,8]{1,0:T(2,128)} %concatenate.43) | copy-start | bytes 196
  155.2 6.3 %copy-start.21 = (f32[8]{0:T(128)S(1)}, f32[8]{0:T(128)}, u32[]{:S(2)}) copy-start(f32[8]{0:T(128)} %param.33) | copy-start | bytes 100
  161.9 1.4 copy-start.2
  162.7 1.7 copy-start.1
  162.7 1.7 copy-start.24
  167.6 0.7 copy-start.22
Sparse Core Ops, SparseCore 0:
  29.9 47.1 all-gather.3
  106.8 40.1 all-gather.5
  167.7 76.7 reduce-scatter.1
where the time goes:
time: 254 us; the launch traced here: 253 us
  waiting for transfers between devices  143 us (56%)
  local copies, waits for them, and re-layouts  36 us (14%)
  matrix products  26.6 us (10%)
  other arithmetic  23.1 us (9%)
  between operations  14.3 us (6%)
  starting transfers between devices  9.98 us (4%)
    reduce_scatter x1, waiting for transfers between devices, on_device(): lax.psum_scatter(jnp.concatenate([partial, side], axis=1).astype(jnp.bflo...  67.9 us
    all_gather x1, waiting for transfers between devices, on_device(): lax.all_gather(jnp.concatenate([block, out_piece], axis=1), 'seq', axis=0...  44.3 us
    all_gather x1, waiting for transfers between devices, on_device(): every = lax.all_gather(sendable, 'seq', axis=0, tiled=False)  21.1 us
    all_to_all x1, waiting for transfers between devices, on_device(): lax.all_to_all(packed, 'tp', split_axis=1, concat_axis=0, tiled=True)  9.66 us
    reshape x2, local copies, waits for them, and re-layouts, on_device(): out_block = gathered[:, width:].reshape(seq_count, out_rows, out_cols)  8.31 us
    all_to_all x1, starting transfers between devices, on_device(): lax.all_to_all(packed, 'tp', split_axis=1, concat_axis=0, tiled=True)  7.7 us
    dot_general x1, matrix products, on_device(): proj = jnp.dot(tokens, weights, preferred_element_type=jnp.float32)  7.02 us
    dot_general x1, matrix products, on_device(): jnp.einsum('jch,jchpn->hpn', own_coef, every_end, precision=lax.Precision...  6.27 us
  transfers between devices with their start and end apart: 5, of which 4 were waited for; matrix products, arithmetic and copies ran while one was open for 14% of the time, Pallas kernels for 0%

commit v1 on v0

--- a/solution.py
+++ b/solution.py
@@ -6,6 +6,13 @@
 INNER = 4096
 GROUP = 256
 epsilon = 1e-05
+
+
+def gather_over(x, mesh_axis, d):
+    peers = lax.axis_size(mesh_axis)
+    shards = jnp.stack([x for _ in range(peers)])
+    shards = lax.all_to_all(shards, mesh_axis, split_axis=0, concat_axis=0)
+    return jnp.concatenate(shards, axis=d)
 
 
 def from_behind(x, axis, by):
@@ -67,9 +74,7 @@
     out_rows, out_cols = w_out.shape
     block_rows = block.shape[0]
     out_piece = w_out.astype(jnp.bfloat16).reshape(block_rows, out_rows * out_cols // block_rows)
-    gathered = lax.all_gather(
-        jnp.concatenate([block, out_piece], axis=1), "seq", axis=0, tiled=True
-    )
+    gathered = gather_over(jnp.concatenate([block, out_piece], axis=1), "seq", 0)
     weights = gathered[:, :width]
     out_block = gathered[:, width:].reshape(seq_count, out_rows, out_cols)
     out_block = out_block.transpose(1, 0, 2).reshape(out_rows, seq_count * out_cols)

time: 254 us -> 337 us (1.33)
  waiting for transfers between devices: 143 us -> 218 us
  starting transfers between devices: 9.98 us -> 14.7 us
  local copies, waits for them, and re-layouts: 36 us -> 40.1 us
    all_to_all x0 -> x1, waiting for transfers between devices: none -> 120 us  [gather_over(): shards = lax.all_to_all(shards, mesh_axis, split_axis=0, concat_axis=0)]
    all_gather x1 -> x0, waiting for transfers between devices: 44.3 us -> none  [on_device(): lax.all_gather(jnp.concatenate([block, out_piece], axis=1), 'seq', axis=0...]
    all_to_all x0 -> x1, starting transfers between devices: none -> 5.22 us  [gather_over(): shards = lax.all_to_all(shards, mesh_axis, split_axis=0, concat_axis=0)]
    another operation x5 -> x6, local copies, waits for them, and re-layouts: 1.05 us -> 5.26 us  [the longest x1 4.21 us: gather_over(): shards = jnp.stack([x for _ in range(peers)])]
    reshape x2 -> x1, local copies, waits for them, and re-layouts: 8.31 us -> 4.35 us  [on_device(): out_block = gathered[:, width:].reshape(seq_count, out_rows, out_cols)]
    transpose x0 -> x1, local copies, waits for them, and re-layouts: none -> 3.96 us  [on_device(): out_block.transpose(1, 0, 2).reshape(out_rows, seq_count * out_cols)]
  transfers between devices with their start and end apart: 5 -> 5, of which waited for: 4 -> 4; matrix products, arithmetic and copies ran while one was open for 14% -> 10% of each run, Pallas kernels for 0% -> 0%
where the time goes in v1:
time: 337 us; the launch traced here: 336 us
  waiting for transfers between devices  218 us (65%)
  local copies, waits for them, and re-layouts  40.1 us (12%)
  matrix products  26.6 us (8%)
  other arithmetic  22.2 us (7%)
  starting transfers between devices  14.7 us (4%)
  between operations  14.5 us (4%)
    all_to_all x1, waiting for transfers between devices, gather_over(): shards = lax.all_to_all(shards, mesh_axis, split_axis=0, concat_axis=0)  120 us
    reduce_scatter x1, waiting for transfers between devices, on_device(): lax.psum_scatter(jnp.concatenate([partial, side], axis=1).astype(jnp.bflo...  68 us
    all_gather x1, waiting for transfers between devices, on_device(): every = lax.all_gather(sendable, 'seq', axis=0, tiled=False)  20.4 us
    all_to_all x1, waiting for transfers between devices, on_device(): lax.all_to_all(packed, 'tp', split_axis=1, concat_axis=0, tiled=True)  9.71 us
    all_to_all x1, starting transfers between devices, on_device(): lax.all_to_all(packed, 'tp', split_axis=1, concat_axis=0, tiled=True)  7.7 us
    dot_general x1, matrix products, on_device(): proj = jnp.dot(tokens, weights, preferred_element_type=jnp.float32)  7.03 us
  transfers between devices with their start and end apart: 5, of which 4 were waited for; matrix products, arithmetic and copies ran while one was open for 10% of the time, Pallas kernels for 0%

profile of v1, /device:TPU:0, one launch (start us, length us, event | category | flops | bytes accessed | tf_op | source)
XLA Modules:
  0.0 336.1 jit_solution(1440642024818572375)
XLA Ops:
  7.2 0.9 convert_element_type.126
  8.1 0.8 copy.116
  9.0 1.1 convert_element_type.125
  10.5 0.8 concatenate.38
  11.4 7.7 %all-to-all-start = ((bf16[16,8,1408]{2,0,1:T(8,128)(2,1)}), bf16[16,8,1408]{2,0,1:T(8,128)(2,1)S(1)}, u32[]{:S(2)}, u32[]{:S(2)}) async-start(bf16[16,8,1408]{2,0,1:T(8,128)(2,1)} %concatenate.38), calls=%async_computation | async-start | bytes 720896 | tf_op jit(solution)/shard_map/all_to_all | solution.py:73
  19.2 9.7 %all-to-all-done = bf16[16,8,1408]{2,0,1:T(8,128)(2,1)S(1)} async-done(((bf16[16,8,1408]{2,0,1:T(8,128)(2,1)}), bf16[16,8,1408]{2,0,1:T(8,128)(2,1)S(1)}, u32[]{:S(2)}, u32[]{:S(2)}) %all-to-all-start) | async-done | bytes 360480 | tf_op jit(solution)/shard_map/all_to_all | solution.py:73
  28.9 4.2 %stack.2 = bf16[16,128,1920]{2,1,0:T(8,128)(2,1)} broadcast(bf16[128,1920]{1,0:T(8,128)(2,1)S(1)} %pad_maximum_fusion.1), dimensions={1,2} | broadcast | bytes 8355840 | tf_op jit(solution)/shard_map/stack | solution.py:13
  33.2 5.2 %all-to-all-start.1 = ((bf16[16,128,1920]{2,1,0:T(8,128)(2,1)}), bf16[16,128,1920]{2,1,0:T(8,128)(2,1)}, u32[]{:S(2)}, u32[]{:S(2)}) async-start(bf16[16,128,1920]{2,1,0:T(8,128)(2,1)} %stack.2), calls=%async_computation.1 | async-start | bytes 15728640 | tf_op jit(solution)/shard_map/all_to_all | solution.py:14
  40.2 0.6 slice_reduce_fusion.5
  41.5 119.8 %all-to-all-done.1 = bf16[16,128,1920]{2,1,0:T(8,128)(2,1)} async-done(((bf16[16,128,1920]{2,1,0:T(8,128)(2,1)}), bf16[16,128,1920]{2,1,0:T(8,128)(2,1)}, u32[]{:S(2)}, u32[]{:S(2)}) %all-to-all-start.1) | async-done | bytes 7864352 | tf_op jit(solution)/shard_map/all_to_all | solution.py:14
  161.3 7.0 %fusion.65 = (bf16[512,1408]{0,1:T(8,128)(2,1)}, f32[512,1408]{0,1:T(8,128)S(1)}) fusion(bf16[512,2048]{1,0:T(8,128)(2,1)S(1)} %copy-done, bf16[2048,1920]{1,0:T(8,128)(2,1)} %bitcast.6), kind=kOutput, calls=%fused_computation.143 | convolution fusion | flops 2953510912 | bytes 12189696 | tf_op jit(solution)/shard_map/dot_general | solution.py:81
  168.5 1.1 reduce-window.19
  169.8 0.7 select_bitcast_fusion
  170.6 1.0 slice.203
  171.7 1.7 collective-permute-start
  173.5 0.7 select_multiply_fusion.1
  174.2 1.2 slice.204
  176.1 0.7 broadcast.363
  176.8 1.4 scatter.11
  178.2 2.9 multiply_convert_fusion.3
  181.1 0.7 fusion.64
  181.9 0.9 reshape.478
  182.9 0.8 copy.123
  183.7 2.0 fusion.29
  185.6 2.8 while.18
  185.7 0.6 fusion.70
  186.3 0.8 bitcast_dynamic-update-slice_fusion.3
  187.1 0.6 fusion.70
  187.7 0.8 bitcast_dynamic-update-slice_fusion.3
  188.5 1.7 pad_maximum_fusion.2
  190.2 0.7 compare_reduce_fusion
  192.1 1.6 compare_and_fusion
  193.7 3.1 slice.226
  196.8 4.3 %reshape.480 = bf16[16,512,128]{2,1,0:T(8,128)(2,1)} reshape(bf16[2048,512]{1,0:T(8,128)(2,1)} %slice.226) | data formatting | bytes 4194304 | tf_op jit(solution)/shard_map/reshape | solution.py:79
  201.1 4.0 %copy.131 = bf16[512,16,128]{0,2,1:T(8,128)(2,1)} copy(bf16[512,16,128]{2,0,1:T(8,128)(2,1)} %bitcast.92) | data formatting | bytes 4194304 | tf_op jit(solution)/shard_map/transpose | solution.py:80
  206.0 3.3 fusion.19
  209.4 20.4 %all-gather.3.cloned.1.call-done = bf16[32,8,72,128]{3,2,1,0:T(8,128)(2,1)} async-done(((bf16[2,8,72,128]{3,2,1,0:T(8,128)(2,1)}), bf16[32,8,72,128]{3,2,1,0:T(8,128)(2,1)}) %all-gather.3.cloned.1.call-update) | async-done | bytes 4718608 | tf_op jit(solution)/shard_map/all_gather | solution.py:167
  229.8 1.5 fusion.63
  231.3 5.7 %slice.224 = bf16[16,2,8,64,128]{4,3,2,1,0:T(8,128)(2,1)} slice(bf16[16,2,8,72,128]{4,3,2,1,0:T(8,128)(2,1)} %bitcast.94), slice={[0:16], [0:2], [0:8], [0:64], [0:128]} | slice | bytes 8388608 | tf_op jit(solution)/shard_map/slice | solution.py:168
  238.0 6.3 %fusion.6 = f32[8,1,64,128,1]{3,1,4,2,0:T(1,128)S(1)} fusion(f32[16,2,8,1,1]{0,3,1,4,2:T(1,128)S(1)} %copy.137, bf16[16,2,8,64,128]{4,3,2,1,0:T(8,128)(2,1)} %slice.224), kind=kOutput, calls=%fused_computation.13 | convolution fusion | flops 25165824 | bytes 4457472 | tf_op jit(solution)/shard_map/jch,jchpn->hpn/dot_general | solution.py:184
  244.7 0.8 copy.130
  247.3 1.6 convolution_convert_fusion
  248.8 1.6 fusion.11
  252.8 5.8 %fusion.22 = f32[2,8,64,128]{3,0,2,1:T(2,128)S(1)} fusion(bf16[16,2,8,64,128]{4,3,2,1,0:T(8,128)(2,1)} %slice.224, f32[2,16,2]{1,0,2:T(2,128)S(1)} %and_convert_fusion, f32[2,16,8]{1,0,2:T(2,128)S(1)} %copy.134, f32[2]{0:T(128)S(1)} %copy-done.23), kind=kOutput, calls=%fused_computation.35 | convolution fusion | flops 50332672 | bytes 4719880 | tf_op jit(solution)/shard_map/rjch,jchpn->rhpn/dot_general | solution.py:225
  258.5 0.9 copy.135
  259.4 68.0 %reduce-scatter.2.cloned.1.call-done = bf16[64,2176]{1,0:T(8,128)(2,1)} async-done(((bf16[512,2176]{1,0:T(8,128)(2,1)}), bf16[64,2176]{1,0:T(8,128)(2,1)}) %reduce-scatter.2.cloned.1.call-update) | async-done | bytes 278544 | tf_op jit(solution)/shard_map/reduce_scatter | solution.py:205
  327.4 1.0 convert_element_type.149
  328.5 0.8 fusion.34
  (134 shorter events, 12.3 us)
Async XLA Ops:
  7.2 154.1 %copy-start = (bf16[512,2048]{1,0:T(8,128)(2,1)S(1)}, bf16[512,2048]{1,0:T(8,128)(2,1)}, u32[]{:S(2)}) copy-start(bf16[512,2048]{1,0:T(8,128)(2,1)} %param.23) | copy-start | bytes 6291460
  7.2 11.9 %copy-start.6 = (f32[512,128]{1,0:T(8,128)S(1)}, f32[512,128]{1,0:T(8,128)}, u32[]{:S(2)}) copy-start(f32[512,128]{1,0:T(8,128)} %param.35) | copy-start | bytes 786436
  11.4 17.5 %all-to-all-start = ((bf16[16,8,1408]{2,0,1:T(8,128)(2,1)}), bf16[16,8,1408]{2,0,1:T(8,128)(2,1)S(1)}, u32[]{:S(2)}, u32[]{:S(2)}) async-start(bf16[16,8,1408]{2,0,1:T(8,128)(2,1)} %concatenate.38), calls=%async_computation | async-start | bytes 720896 | tf_op jit(solution)/shard_map/all_to_all | solution.py:73
  33.1 5.3 %copy-start.25 = (s32[8]{0:T(128)S(1)}, s32[8]{0:T(128)}, u32[]{:S(2)}) copy-start(s32[8]{0:T(128)} %param.36) | copy-start | bytes 100
  33.1 6.2 %copy-start.16 = (f32[512]{0:T(512)S(1)}, f32[512]{0:T(512)}, u32[]{:S(2)}) copy-start(f32[512]{0:T(512)} %param.28) | copy-start | bytes 6148
  33.2 6.2 %copy-start.19 = (f32[256]{0:T(256)S(1)}, f32[256]{0:T(256)}, u32[]{:S(2)}) copy-start(f32[256]{0:T(256)} %param.30) | copy-start | bytes 3076
  33.2 6.8 %copy-start.11 = (f32[4,512]{1,0:T(4,128)S(1)}, f32[4,512]{1,0:T(4,128)}, u32[]{:S(2)}) copy-start(f32[4,512]{1,0:T(4,128)} %param.27) | copy-start | bytes 24580
  33.2 6.8 %copy-start.13 = (f32[4,256]{1,0:T(4,128)S(1)}, f32[4,256]{1,0:T(4,128)}, u32[]{:S(2)}) copy-start(f32[4,256]{1,0:T(4,128)} %param.29) | copy-start | bytes 12292
  33.2 7.6 %copy-start.26 = (f32[8]{0:T(128)S(1)}, f32[8]{0:T(128)}, u32[]{:S(2)}) copy-start(f32[8]{0:T(128)} %param.32) | copy-start | bytes 100
  33.2 128.1 %all-to-all-start.1 = ((bf16[16,128,1920]{2,1,0:T(8,128)(2,1)}), bf16[16,128,1920]{2,1,0:T(8,128)(2,1)}, u32[]{:S(2)}, u32[]{:S(2)}) async-start(bf16[16,128,1920]{2,1,0:T(8,128)(2,1)} %stack.2), calls=%async_computation.1 | async-start | bytes 15728640 | tf_op jit(solution)/shard_map/all_to_all | solution.py:14
  38.4 191.4 %all-gather.3.cloned.1.call-start = ((), (), s32[]{:S(2)}) async-start(), calls=%async_computation.4 | async-start | bytes 5013504 | tf_op jit(solution)/shard_map/all_gather | solution.py:167
  39.2 129.1 %copy-start.9 = (s32[2,256]{1,0:T(2,128)}, s32[2,256]{1,0:T(2,128)S(1)}, u32[]{:S(2)}) copy-start(s32[2,256]{1,0:T(2,128)S(1)} %eq.111) | copy-start | bytes 6148
  161.3 7.0 %copy-start.20 = (f32[8]{0:T(128)S(1)}, f32[8]{0:T(128)}, u32[]{:S(2)}) copy-start(f32[8]{0:T(128)} %param.31) | copy-start | bytes 100
  170.5 3.7 %copy-start.7 = (f32[2,8,256]{2,1,0:T(8,128)}, f32[2,8,256]{2,1,0:T(8,128)S(1)}, u32[]{:S(2)}) copy-start(f32[2,8,256]{2,1,0:T(8,128)S(1)} %get-tuple-element.130) | copy-start | bytes 49156
  171.7 6.5 %collective-permute-start = (bf16[3,768]{0,1:T(8,128)(2,1)S(1)}, bf16[3,768]{0,1:T(8,128)(2,1)S(1)}, u32[]{:S(2)}, u32[]{:S(2)}) collective-permute-start(bf16[3,768]{0,1:T(8,128)(2,1)S(1)} %slice.203), channel_id=1, source_target_pairs={{0,8},{8,16},{16,24},{24,32},{32,40},{40,48},{48,56},{56,64},{64,7... | collective-permute-start | bytes 13832 | tf_op jit(solution)/shard_map/ppermute | solution.py:21
  173.5 0.7 copy-start.15
  173.5 0.7 copy-start.14
  190.2 137.2 %reduce-scatter.2.cloned.1.call-start = ((), (), s32[]{:S(2)}) async-start(), calls=%async_computation.3 | async-start | bytes 2506752 | tf_op jit(solution)/shard_map/reduce_scatter | solution.py:205
  190.9 0.6 copy-start.17
  201.1 4.0 %slice-start = ((f32[2,8]{1,0:T(2,128)}), f32[1,8]{1,0:T(1,128)S(1)}, s32[]{:S(2)}) async-start(f32[2,8]{1,0:T(2,128)} %copy-done.14), calls=%async_computation.5 | async-start | bytes 1024 | tf_op jit(solution)/shard_map/slice | solution.py:155
  201.1 4.6 %copy-start.3 = (bf16[512,128]{0,1:T(8,128)(2,1)S(1)}, bf16[512,128]{0,1:T(8,128)(2,1)}, u32[]{:S(2)}) copy-start(bf16[512,128]{0,1:T(8,128)(2,1)} %get-tuple-element.135) | copy-start | bytes 393220
  231.3 6.1 %copy-start.10 = (pred[16,16]{1,0:T(8,128)(4,1)S(1)}, pred[16,16]{1,0:T(8,128)(4,1)}, u32[]{:S(2)}) copy-start(pred[16,16]{1,0:T(8,128)(4,1)} %broadcast_and_fusion.1) | copy-start | bytes 772
  231.3 6.5 %copy-start.18 = (pred[16]{0:T(512)(128)(4,1)S(1)}, pred[16]{0:T(512)(128)(4,1)}, u32[]{:S(2)}) copy-start(pred[16]{0:T(512)(128)(4,1)} %copy-done.17) | copy-start | bytes 52
  231.3 6.5 %copy-start.23 = (f32[2]{0:T(128)S(1)}, f32[2]{0:T(128)}, u32[]{:S(2)}) copy-start(f32[2]{0:T(128)} %compare_convert_fusion) | copy-start | bytes 28
  238.0 6.3 %copy-start.4 = (f32[2,256,8,64]{1,3,2,0:T(8,128)S(1)}, f32[2,256,8,64]{1,3,2,0:T(8,128)}, u32[]{:S(2)}) copy-start(f32[2,256,8,64]{1,3,2,0:T(8,128)} %fusion.19) | copy-start | bytes 3145732
  238.0 6.3 %copy-start.5 = (f32[2,8,64,128]{3,2,1,0:T(8,128)S(1)}, f32[2,8,64,128]{3,2,1,0:T(8,128)}, u32[]{:S(2)}) copy-start(f32[2,8,64,128]{3,2,1,0:T(8,128)} %get-tuple-element.72) | copy-start | bytes 1572868
  238.0 6.3 %copy-start.8 = (f32[2,256,8]{1,2,0:T(8,128)S(1)}, f32[2,256,8]{1,2,0:T(8,128)}, u32[]{:S(2)}) copy-start(f32[2,256,8]{1,2,0:T(8,128)} %get-tuple-element.129) | copy-start | bytes 49156
  238.0 6.3 %copy-start.12 = (f32[2,8]{1,0:T(2,128)S(1)}, f32[2,8]{1,0:T(2,128)}, u32[]{:S(2)}) copy-start(f32[2,8]{1,0:T(2,128)} %concatenate.43) | copy-start | bytes 196
  238.0 6.3 %copy-start.21 = (f32[8]{0:T(128)S(1)}, f32[8]{0:T(128)}, u32[]{:S(2)}) copy-start(f32[8]{0:T(128)} %param.33) | copy-start | bytes 100
  244.7 1.4 copy-start.2
  245.6 1.7 copy-start.1
  245.6 1.7 copy-start.24
  250.4 0.7 copy-start.22
Sparse Core Ops, SparseCore 0:
  190.3 39.4 all-gather.2
  250.5 76.7 reduce-scatter.1
